TPU v7x, 768 devices: a whole 4x8x12 slice. The times are simulated.
768 devices in a mesh: mom: 24 (over z_hi, y), trow: 4 (over z_lo), tcol: 8 (over x, core).
Axes of the slice: x: 4, y: 8, z: 12 (z_hi: 3, z_lo: 4; z = z_hi * 4 + z_lo), core: 2. Of those that a mesh axis runs over, the one named last changes fastest.
Arguments:
- g_free: float32 [2, 24, 1536, 1536], P(None, 'mom', 'tcol', 'trow'), may hold values from -6 to 6
- g_greater_t: float32 [2, 24, 1536, 1536], P(None, 'mom', 'tcol', 'trow'), may hold values from -6 to 6
- momentum_map: int32 [24], replicated, may hold values from 0 to 23, each once
- weights: float32 [1536], replicated, may hold values from 0.00076546555 to 0.0076546553
Outputs:
- g_out: float32 [2, 24, 1536, 1536], P(None, 'mom', 'tcol', 'trow')
Inputs may be any that keep to these rules, and one draw needn't show every extreme that they name: `momentum_map`: each number appears once.
All inputs are finite; a program needn't handle non-finite values.
Results may differ from a plain program's by a relative error of at most 0.00022.
Values sent between devices are 32-bit elements; how exact they have to be, the bound alone decides.
No kernel may reach another device: no remote copies, remote signals or barrier semaphores. Data moves between devices by JAX's collectives and lax.ppermute only.
A program may use at most 32 MiB of HBM per device.

v0:
```python
import math

import jax
import jax.numpy as jnp
from jax import lax
from jax.experimental import pallas as pl
from jax.experimental.pallas import tpu as pltpu
from jax.sharding import Mesh, PartitionSpec as P


ITERS = 2


CHUNKS = 2
VMEM = 24 * 1024 * 1024

LANES = 128
ROOT3_2 = math.sqrt(3.0) / 2.0


def c_add(a, b):
    return (a[0] + b[0], a[1] + b[1])


def c_sub(a, b):
    return (a[0] - b[0], a[1] - b[1])


def c_turn(a, sign):
    return (-a[1], a[0]) if sign > 0 else (a[1], -a[0])


def dft3(x0, x1, x2, sign):
    u = c_add(x1, x2)
    v = c_sub(x1, x2)
    m = (x0[0] - 0.5 * u[0], x0[1] - 0.5 * u[1])
    n = c_turn((ROOT3_2 * v[0], ROOT3_2 * v[1]), sign)
    return c_add(x0, u), c_add(m, n), c_sub(m, n)


def dft4(x, sign):
    t0, t1 = c_add(x[0], x[2]), c_sub(x[0], x[2])
    t2, t3 = c_add(x[1], x[3]), c_turn(c_sub(x[1], x[3]), sign)
    return [c_add(t0, t2), c_add(t1, t3), c_sub(t0, t2), c_sub(t1, t3)]


def dft6(x, sign):
    b = [c_add(x[m], x[m + 3]) for m in range(3)]
    c = [c_sub(x[m], x[m + 3]) for m in range(3)]
    even = dft3(b[0], b[1], b[2], sign)
    odd = dft3(c[0], (-c[1][0], -c[1][1]), c[2], sign)
    return [even[0], odd[2], even[1], odd[0], even[2], odd[1]]


def lattice_transform(x, sign):
    rows = [[None] * 6 for _ in range(4)]
    for across in range(6):
        column = dft4([x[6 * down + across] for down in range(4)], sign)
        for down in range(4):
            rows[down][across] = column[down]
    out = []
    for down in range(4):
        out.extend(dft6(rows[down], sign))
    return out


def self_energy_kernel(first, map_ref, weights_ref, field_ref, *refs):
    if first:
        sigma_ref, mirror_ref, where_ref = refs
    else:
        mirror_ref, sigma_ref, where_ref = refs
    momenta = field_ref.shape[0]
    for k in range(momenta):
        where_ref[map_ref[k]] = k
    spot = [where_ref[q] for q in range(momenta)]
    zl = lax.axis_index("zl")
    for lane in range(0, field_ref.shape[3], LANES):
        cut = pl.ds(lane, LANES)
        if first:
            mirror = lattice_transform(
                [(field_ref[k, 2, :, cut], field_ref[k, 3, :, cut]) for k in spot], -1
            )
            scale = 1.0 / (momenta * momenta)
            for r in range(momenta):
                mirror_ref[r, 0, :, cut] = mirror[r][0] * scale
                mirror_ref[r, 1, :, cut] = mirror[r][1] * scale
        space = lattice_transform(
            [(field_ref[k, 0, :, cut], field_ref[k, 1, :, cut]) for k in spot], 1
        )
        source = []
        for r in range(momenta):
            re, im = space[r]
            sq_re = re * re - im * im
            sq_im = 2.0 * re * im
            m_re, m_im = mirror_ref[r, 0, :, cut], mirror_ref[r, 1, :, cut]
            source.append((sq_re * m_re - sq_im * m_im, sq_re * m_im + sq_im * m_re))
        sigma = lattice_transform(source, -1)
        w = weights_ref[zl, :, cut]
        for q in range(momenta):
            sigma_ref[spot[q], 0, :, cut] = sigma[q][0] * w
            sigma_ref[spot[q], 1, :, cut] = sigma[q][1] * w


def self_energy(momentum_map, weights, field, mirror=None):
    first = mirror is None
    momenta, _, rows, cols = field.shape
    shape = jax.ShapeDtypeStruct((momenta, 2, rows, cols), jnp.float32)
    smem = pl.BlockSpec(memory_space=pltpu.SMEM)
    vmem = pl.BlockSpec(memory_space=pltpu.VMEM)
    ins = [momentum_map, weights, field] + ([] if first else [mirror])
    return pl.pallas_call(
        lambda *refs: self_energy_kernel(first, *refs),
        out_shape=(shape, shape) if first else shape,
        in_specs=[smem] + [vmem] * (len(ins) - 1),
        out_specs=(vmem, vmem) if first else vmem,
        scratch_shapes=[pltpu.SMEM((momenta,), jnp.int32)],
        compiler_params=pltpu.CompilerParams(vmem_limit_bytes=VMEM),
        name="self_energy_first" if first else "self_energy_next",
    )(*ins)


def split_left(x):
    hi = x.astype(jnp.bfloat16)
    lo = (x - hi.astype(jnp.float32)).astype(jnp.bfloat16)
    return jnp.concatenate([hi, lo, hi], axis=1)


def split_right(x):
    hi = x.astype(jnp.bfloat16)
    lo = (x - hi.astype(jnp.float32)).astype(jnp.bfloat16)
    return jnp.concatenate([hi, hi, lo], axis=0)


def mul(a, b):
    return jnp.dot(split_left(a), split_right(b), preferred_element_type=jnp.float32)


def product_kernel(n_lefts, blocks_ref, *refs):
    lefts, panels, refs = refs[:n_lefts], refs[n_lefts : 2 * n_lefts], refs[2 * n_lefts :]
    out_ref = refs[-1]

    def flat(x):
        return x.reshape(x.shape[0] * x.shape[1], x.shape[2])

    re = im = None
    if len(refs) == 2:
        re, im = refs[0][0], refs[0][1]
    for left_ref, panel_ref in zip(lefts, panels):
        s_re, s_im = flat(left_ref[:, 0]), flat(left_ref[:, 1])
        g_re, g_im = flat(panel_ref[:, 0]), flat(panel_ref[:, 1])
        one = mul(s_re, g_re)
        two = mul(s_im, g_im)
        three = mul(s_re + s_im, g_re + g_im)
        if re is None:
            re, im = one - two, three - one - two
        else:
            re, im = re + (one - two), im + (three - one - two)
    out_ref[0] = re
    out_ref[1] = im


def product(lefts, panel, blocks, base=None, chunk=0):
    slabs, _, high, cols = lefts[0].shape
    rows = slabs * high
    per = cols // panel.shape[2]
    full = lambda shape: pl.BlockSpec(shape, lambda i, b: (0,) * len(shape))
    in_specs = [full(x.shape) for x in lefts]
    for j in range(len(lefts)):
        in_specs.append(
            pl.BlockSpec((per,) + panel.shape[1:], lambda i, b, j=j: (b[j], 0, 0, 0))
        )
    ins = list(lefts) + [panel] * len(lefts)
    if base is not None:
        in_specs.append(pl.BlockSpec((2, rows, cols), lambda i, b: (0, chunk, 0)))
        ins.append(base)
    return pl.pallas_call(
        lambda *refs: product_kernel(len(lefts), *refs),
        out_shape=jax.ShapeDtypeStruct((2, rows, cols), jnp.float32),
        grid_spec=pltpu.PrefetchScalarGridSpec(
            num_scalar_prefetch=1,
            grid=(1,),
            in_specs=in_specs,
            out_specs=full((2, rows, cols)),
        ),
        compiler_params=pltpu.CompilerParams(vmem_limit_bytes=VMEM),
        name="product_other" if base is None else "product_own",
    )(blocks, *ins)


def finish_kernel(n, tiled, *refs):
    own, other, outs = refs[:n], refs[n : 2 * n], refs[2 * n :]
    rows = own[0].shape[1]
    for i in range(n):
        for j in range(2):
            x = own[i][j] + other[i][j]
            outs[0][j, i * rows : (i + 1) * rows] = x
            if tiled:
                slabs, _, high, cols = outs[1].shape
                outs[1][i * slabs // n : (i + 1) * slabs // n, j] = x.reshape(
                    slabs // n, high, cols
                )


def finish(own, other, tiles):
    n = len(own)
    _, rows, cols = own[0].shape
    outs = [jax.ShapeDtypeStruct((2, n * rows, cols), jnp.float32)]
    if tiles is not None:
        outs.append(jax.ShapeDtypeStruct(tiles, jnp.float32))
    vmem = pl.BlockSpec(memory_space=pltpu.VMEM)
    return pl.pallas_call(
        lambda *refs: finish_kernel(n, tiles is not None, *refs),
        out_shape=outs,
        in_specs=[vmem] * (2 * n),
        out_specs=[vmem] * len(outs),
        compiler_params=pltpu.CompilerParams(vmem_limit_bytes=VMEM),
        name="finish_tiled" if tiles is not None else "finish",
    )(*own, *other)


def time_product(sigma, panel, free, tiled):
    zl = lax.axis_index("zl")
    turn = lambda by: lax.bitwise_xor(zl, by)
    own_blocks = jnp.stack([zl, turn(2)])
    other_blocks = jnp.stack([turn(1), turn(3)])
    slabs = sigma.shape[0] // CHUNKS
    mine = [sigma[i * slabs : (i + 1) * slabs] for i in range(CHUNKS)]
    swapped = [lax.ppermute(x, "zl", [(0, 2), (1, 3), (2, 0), (3, 1)]) for x in mine]
    own, other = [], []
    for i, (left, right) in enumerate(zip(mine, swapped)):
        if own:
            right, own[-1], _ = lax.optimization_barrier((right, own[-1], part))
        pair = (left, right)
        part = product(pair, panel, other_blocks)
        other.append(lax.ppermute(part, "zl", [(0, 1), (1, 0), (2, 3), (3, 2)]))
        own.append(product(pair, panel, own_blocks, free, i))
    return finish(own, other, sigma.shape if tiled else None)


def pack_kernel(free_ref, greater_ref, out_ref):
    for j in range(2):
        out_ref[:, j] = free_ref[j]
        out_ref[:, 2 + j] = greater_ref[j]


def pack(free, greater):
    _, slabs, high, cols = free.shape
    step = slabs // 4
    block = pl.BlockSpec((2, step, high, cols), lambda i: (0, i, 0, 0))
    return pl.pallas_call(
        pack_kernel,
        out_shape=jax.ShapeDtypeStruct((slabs, 4, high, cols), jnp.float32),
        grid=(4,),
        in_specs=[block, block],
        out_specs=pl.BlockSpec((step, 4, high, cols), lambda i: (i, 0, 0, 0)),
        compiler_params=pltpu.CompilerParams(vmem_limit_bytes=VMEM),
        name="pack",
    )(*(pltpu.with_memory_space_constraint(x, pltpu.HBM) for x in (free, greater)))


def exchange(x):
    return lax.all_to_all(x, ("zh", "y"), 0, 0, tiled=True)


def spread(tile):
    nx = lax.axis_size("x")
    moves = []
    for zl in range(lax.axis_size("zl")):
        for x in range(nx):
            stays = x % 2 == zl % 2
            to = (zl, x) if stays else (zl ^ 1, x ^ 1)
            moves.append((zl * nx + x, to[0] * nx + to[1]))
    return lax.ppermute(tile, ("zl", "x"), moves)


def body(g_free, g_greater_t, momentum_map, weights):
    momenta = momentum_map.shape[0]
    free, greater = g_free[:, 0], g_greater_t[:, 0]
    tile_rows, tile_cols = free.shape[1:]
    slabs = (2, momenta, tile_rows // momenta, tile_cols)
    weights = weights.reshape(-1, 1, tile_cols)

    moved = spread(free)
    both = pack(free.reshape(slabs), greater.reshape(slabs))
    field = exchange(both)
    mirror = None
    for sweep in range(ITERS):
        moved = settle(moved)
        panel = lax.all_gather(moved, ("x", "core"))
        panel = pltpu.with_memory_space_constraint(panel, pltpu.HBM)
        if mirror is None:
            sigma, mirror = self_energy(momentum_map, weights, field)
        else:
            sigma = self_energy(momentum_map, weights, field, mirror)
        sigma = exchange(sigma)
        if sweep == ITERS - 1:
            return time_product(sigma, panel, free, False)[0][:, None]
        green, tiles = time_product(sigma, panel, free, True)
        moved = spread(green)
        field = exchange(tiles)


def settle(tile):
    def kernel(tile_ref, out_ref):
        out_ref[...] = tile_ref[...]

    return pl.pallas_call(
        kernel,
        out_shape=jax.ShapeDtypeStruct(tile.shape, tile.dtype),
        compiler_params=pltpu.CompilerParams(vmem_limit_bytes=VMEM),
        name="settle",
    )(tile)


def solution(mesh):
    fine = Mesh(mesh.devices.reshape(3, 8, 4, 4, 2), ("zh", "y", "zl", "x", "core"))
    spec = P(None, ("zh", "y"), ("x", "core"), "zl")
    return jax.shard_map(
        body, mesh=fine, in_specs=(spec, spec, P(), P()), out_specs=spec, check_vma=False
    )
```

profile of v0, /device:TPU:1, one launch (start us, length us, event | category | flops | bytes accessed | tf_op | source)
XLA Modules:
  0.0 289.5 jit_solution(7845817765146750017)
XLA Ops:
  6.5 1.8 collective-permute-start.2
  8.4 0.9 settle.2
  9.3 3.5 %pack.1 = f32[24,4,8,384]{3,2,1,0:T(8,128)} custom-call(f32[2,24,8,384]{3,2,1,0:T(8,128)} %bitcast.13, f32[2,24,8,384]{3,2,1,0:T(8,128)} %bitcast.34), custom_call_target="tpu_custom_call" | custom-call | tf_op jit(solution)/shard_map/pack/pallas_call | solution.py:250
  12.8 20.0 %all-to-all-start = ((f32[24,4,8,384]{3,2,1,0:T(8,128)}), f32[24,4,8,384]{3,2,1,0:T(8,128)S(1)}, u32[]{:S(2)}, u32[]{:S(2)}) async-start(f32[24,4,8,384]{3,2,1,0:T(8,128)} %pack.1), calls=%async_computation | async-start | bytes 2359296 | tf_op jit(solution)/shard_map/all_to_all | solution.py:262
  32.8 30.7 %all-to-all-done.refs_2_ = f32[24,4,8,384]{3,2,1,0:T(8,128)S(1)} async-done(((f32[24,4,8,384]{3,2,1,0:T(8,128)}), f32[24,4,8,384]{3,2,1,0:T(8,128)S(1)}, u32[]{:S(2)}, u32[]{:S(2)}) %all-to-all-start) | async-done | bytes 1179680 | tf_op jit(solution)/shard_map/all_to_all | solution.py:262
  63.6 1.1 self_energy_first.1
  64.7 45.8 %all_to_all.20 = f32[24,2,8,384]{3,2,1,0:T(8,128)S(1)} all-to-all(f32[24,2,8,384]{3,2,1,0:T(8,128)S(1)} %get-tuple-element.13), channel_id=1, replica_groups=mesh['zh'=3,'y'=8,'zl'=4,'x'=4,'core'=2] {'zh','y'}, dimensions={0} | all-to-all | bytes 1179648 | tf_op jit(solution)/shard_map/all_to_all | solution.py:262
  110.6 12.0 %collective-permute-start.1 = (f32[12,2,8,384]{3,2,1,0:T(8,128)S(1)}, f32[12,2,8,384]{3,2,1,0:T(8,128)S(1)}, u32[]{:S(2)}, u32[]{:S(2)}) collective-permute-start(f32[12,2,8,384]{3,2,1,0:T(8,128)S(1)} %get-tuple-element.23.refs_1_), channel_id=1, source_target_pairs={{0,16},{8,24},{16,0},{24,8},{1,17},{9,25},{17,1},{25,9},{2,18},{10... | collective-permute-start | bytes 884744 | tf_op jit(solution)/shard_map/ppermute | solution.py:228
  122.6 1.9 collective-permute-start
  124.7 17.3 %collective-permute-done.1.refs_2_ = f32[12,2,8,384]{3,2,1,0:T(8,128)S(1)} collective-permute-done((f32[12,2,8,384]{3,2,1,0:T(8,128)S(1)}, f32[12,2,8,384]{3,2,1,0:T(8,128)S(1)}, u32[]{:S(2)}, u32[]{:S(2)}) %collective-permute-start.1) | collective-permute-done | bytes 294944 | tf_op jit(solution)/shard_map/ppermute | solution.py:228
  142.0 3.2 %product_other.4 = f32[2,96,384]{2,1,0:T(8,128)S(1)} custom-call(s32[2]{0:T(128)S(1)} %pad_add_fusion.1.refs_0_, f32[12,2,8,384]{3,2,1,0:T(8,128)S(1)} %get-tuple-element.23.refs_1_, f32[12,2,8,384]{3,2,1,0:T(8,128)S(1)} %collective-permute-done.1.refs_2_, f32[8,2,192,384]{3,2,1,0:T(8,128)} %bitcast.18, f32[8,2,192,384]{3,2,1,0:T(8,128)} %bitcast.19), custom_call_target="tpu_custom_call" | custom-call | tf_op jit(solution)/shard_map/product_other/pallas_call | solution.py:176
  145.2 3.1 %collective-permute-start.3 = (f32[2,96,384]{2,1,0:T(8,128)S(1)}, f32[2,96,384]{2,1,0:T(8,128)S(1)}, u32[]{:S(2)}, u32[]{:S(2)}) collective-permute-start(f32[2,96,384]{2,1,0:T(8,128)S(1)} %product_other.4), channel_id=1, source_target_pairs={{0,8},{8,0},{16,24},{24,16},{1,9},{9,1},{17,25},{25,17},{2,10},{10... | collective-permute-start | bytes 884744 | tf_op jit(solution)/shard_map/ppermute | solution.py:235
  148.3 3.2 %product_own.4.refs_0_ = f32[2,96,384]{2,1,0:T(8,128)S(1)} custom-call(s32[2]{0:T(128)S(1)} %pad_add_fusion.refs_0_, f32[12,2,8,384]{3,2,1,0:T(8,128)S(1)} %get-tuple-element.23.refs_1_, f32[12,2,8,384]{3,2,1,0:T(8,128)S(1)} %collective-permute-done.1.refs_2_, f32[8,2,192,384]{3,2,1,0:T(8,128)} %bitcast.20, f32[8,2,192,384]{3,2,1,0:T(8,128)} %bitcast.21, ...), custom_call_target="tpu_custom_call" | custom-call | tf_op jit(solution)/shard_map/product_own/pallas_call | solution.py:176
  151.6 3.3 %product_other.5 = f32[2,96,384]{2,1,0:T(8,128)S(1)} custom-call(s32[2]{0:T(128)S(1)} %pad_add_fusion.1.refs_0_, f32[12,2,8,384]{3,2,1,0:T(8,128)S(1)} %get-tuple-element.24.refs_1_, f32[12,2,8,384]{3,2,1,0:T(8,128)S(1)} %collective-permute-done.refs_2_, f32[8,2,192,384]{3,2,1,0:T(8,128)} %bitcast.22, f32[8,2,192,384]{3,2,1,0:T(8,128)} %bitcast.23), custom_call_target="tpu_custom_call" | custom-call | tf_op jit(solution)/shard_map/product_other/pallas_call | solution.py:176
  154.9 2.2 collective-permute-start.4
  157.1 3.2 %product_own.5.refs_1_ = f32[2,96,384]{2,1,0:T(8,128)S(1)} custom-call(s32[2]{0:T(128)S(1)} %pad_add_fusion.refs_0_, f32[12,2,8,384]{3,2,1,0:T(8,128)S(1)} %get-tuple-element.24.refs_1_, f32[12,2,8,384]{3,2,1,0:T(8,128)S(1)} %collective-permute-done.refs_2_, f32[8,2,192,384]{3,2,1,0:T(8,128)} %bitcast.24, f32[8,2,192,384]{3,2,1,0:T(8,128)} %bitcast.25, ...), custom_call_target="tpu_custom_call" | custom-call | tf_op jit(solution)/shard_map/product_own/pallas_call | solution.py:176
  160.3 4.1 %collective-permute-done.4.refs_3_ = f32[2,96,384]{2,1,0:T(8,128)S(1)} collective-permute-done((f32[2,96,384]{2,1,0:T(8,128)S(1)}, f32[2,96,384]{2,1,0:T(8,128)S(1)}, u32[]{:S(2)}, u32[]{:S(2)}) %collective-permute-start.4) | collective-permute-done | bytes 294944 | tf_op jit(solution)/shard_map/ppermute | solution.py:235
  165.2 0.9 settle.3
  166.1 21.5 %all_to_all.21.refs_2_ = f32[24,2,8,384]{3,2,1,0:T(8,128)S(1)} all-to-all(f32[24,2,8,384]{3,2,1,0:T(8,128)S(1)} %get-tuple-element.16), channel_id=1, replica_groups=mesh['zh'=3,'y'=8,'zl'=4,'x'=4,'core'=2] {'zh','y'}, dimensions={0} | all-to-all | bytes 1179648 | tf_op jit(solution)/shard_map/all_to_all | solution.py:262
  187.6 1.0 self_energy_next.1
  188.6 28.0 %all_to_all.22 = f32[24,2,8,384]{3,2,1,0:T(8,128)S(1)} all-to-all(f32[24,2,8,384]{3,2,1,0:T(8,128)S(1)} %self_energy_next.1), channel_id=1, replica_groups=mesh['zh'=3,'y'=8,'zl'=4,'x'=4,'core'=2] {'zh','y'}, dimensions={0} | all-to-all | bytes 1179648 | tf_op jit(solution)/shard_map/all_to_all | solution.py:262
  216.6 11.1 %collective-permute-start.6 = (f32[12,2,8,384]{3,2,1,0:T(8,128)S(1)}, f32[12,2,8,384]{3,2,1,0:T(8,128)S(1)}, u32[]{:S(2)}, u32[]{:S(2)}) collective-permute-start(f32[12,2,8,384]{3,2,1,0:T(8,128)S(1)} %get-tuple-element.21.refs_1_), channel_id=1, source_target_pairs={{0,16},{8,24},{16,0},{24,8},{1,17},{9,25},{17,1},{25,9},{2,18},{10... | collective-permute-start | bytes 884744 | tf_op jit(solution)/shard_map/ppermute | solution.py:228
  227.7 1.9 collective-permute-start.5
  229.6 10.7 %collective-permute-done.6.refs_2_ = f32[12,2,8,384]{3,2,1,0:T(8,128)S(1)} collective-permute-done((f32[12,2,8,384]{3,2,1,0:T(8,128)S(1)}, f32[12,2,8,384]{3,2,1,0:T(8,128)S(1)}, u32[]{:S(2)}, u32[]{:S(2)}) %collective-permute-start.6) | collective-permute-done | bytes 294944 | tf_op jit(solution)/shard_map/ppermute | solution.py:228
  240.4 3.2 %product_other.6 = f32[2,96,384]{2,1,0:T(8,128)S(1)} custom-call(s32[2]{0:T(128)S(1)} %pad_add_fusion.1.refs_0_, f32[12,2,8,384]{3,2,1,0:T(8,128)S(1)} %get-tuple-element.21.refs_1_, f32[12,2,8,384]{3,2,1,0:T(8,128)S(1)} %collective-permute-done.6.refs_2_, f32[8,2,192,384]{3,2,1,0:T(8,128)} %bitcast.26, f32[8,2,192,384]{3,2,1,0:T(8,128)} %bitcast.27), custom_call_target="tpu_custom_call" | custom-call | tf_op jit(solution)/shard_map/product_other/pallas_call | solution.py:176
  243.6 3.2 %product_own.6.refs_0_ = f32[2,96,384]{2,1,0:T(8,128)S(1)} custom-call(s32[2]{0:T(128)S(1)} %pad_add_fusion.refs_0_, f32[12,2,8,384]{3,2,1,0:T(8,128)S(1)} %get-tuple-element.21.refs_1_, f32[12,2,8,384]{3,2,1,0:T(8,128)S(1)} %collective-permute-done.6.refs_2_, f32[8,2,192,384]{3,2,1,0:T(8,128)} %bitcast.28, f32[8,2,192,384]{3,2,1,0:T(8,128)} %bitcast.29, ...), custom_call_target="tpu_custom_call" | custom-call | tf_op jit(solution)/shard_map/product_own/pallas_call | solution.py:176
  246.9 3.2 %product_other.7 = f32[2,96,384]{2,1,0:T(8,128)S(1)} custom-call(s32[2]{0:T(128)S(1)} %pad_add_fusion.1.refs_0_, f32[12,2,8,384]{3,2,1,0:T(8,128)S(1)} %get-tuple-element.22.refs_1_, f32[12,2,8,384]{3,2,1,0:T(8,128)S(1)} %collective-permute-done.5.refs_2_, f32[8,2,192,384]{3,2,1,0:T(8,128)} %bitcast.30, f32[8,2,192,384]{3,2,1,0:T(8,128)} %bitcast.31), custom_call_target="tpu_custom_call" | custom-call | tf_op jit(solution)/shard_map/product_other/pallas_call | solution.py:176
  250.1 22.6 %collective-permute-start.9 = (f32[2,96,384]{2,1,0:T(8,128)S(1)}, f32[2,96,384]{2,1,0:T(8,128)S(1)}, u32[]{:S(2)}, u32[]{:S(2)}) collective-permute-start(f32[2,96,384]{2,1,0:T(8,128)S(1)} %product_other.7), channel_id=1, source_target_pairs={{0,8},{8,0},{16,24},{24,16},{1,9},{9,1},{17,25},{25,17},{2,10},{10... | collective-permute-start | bytes 884744 | tf_op jit(solution)/shard_map/ppermute | solution.py:235
  272.8 1.9 collective-permute-start.8
  274.7 3.2 %product_own.7.refs_1_ = f32[2,96,384]{2,1,0:T(8,128)S(1)} custom-call(s32[2]{0:T(128)S(1)} %pad_add_fusion.refs_0_, f32[12,2,8,384]{3,2,1,0:T(8,128)S(1)} %get-tuple-element.22.refs_1_, f32[12,2,8,384]{3,2,1,0:T(8,128)S(1)} %collective-permute-done.5.refs_2_, f32[8,2,192,384]{3,2,1,0:T(8,128)} %bitcast.32, f32[8,2,192,384]{3,2,1,0:T(8,128)} %bitcast.33, ...), custom_call_target="tpu_custom_call" | custom-call | tf_op jit(solution)/shard_map/product_own/pallas_call | solution.py:176
  277.9 3.9 %collective-permute-done.8.refs_2_ = f32[2,96,384]{2,1,0:T(8,128)S(1)} collective-permute-done((f32[2,96,384]{2,1,0:T(8,128)S(1)}, f32[2,96,384]{2,1,0:T(8,128)S(1)}, u32[]{:S(2)}, u32[]{:S(2)}) %collective-permute-start.8) | collective-permute-done | bytes 294944 | tf_op jit(solution)/shard_map/ppermute | solution.py:235
  281.8 0.9 finish.1
  (25 shorter events, 1.1 us)
Async XLA Ops:
  6.5 26.3 %copy-start.2 = (f32[1536]{0:T(1024)S(1)}, f32[1536]{0:T(1024)}, u32[]{:S(2)}) copy-start(f32[1536]{0:T(1024)} %param.7) | copy-start | bytes 18436
  6.5 57.0 %copy-start.1 = (s32[24]{0:T(128)S(1)}, s32[24]{0:T(128)}, u32[]{:S(2)}) copy-start(s32[24]{0:T(128)} %refs_0_.3) | copy-start | bytes 292
  6.5 135.5 %all-gather.5.cloned.1.call-start = ((), (), s32[]{:S(2)}) async-start(), calls=%async_computation.4 | async-start | bytes 5308416 | tf_op jit(solution)/shard_map/all_gather | solution.py:289
  6.5 1.8 collective-permute-start.2
  12.8 50.8 %all-to-all-start = ((f32[24,4,8,384]{3,2,1,0:T(8,128)}), f32[24,4,8,384]{3,2,1,0:T(8,128)S(1)}, u32[]{:S(2)}, u32[]{:S(2)}) async-start(f32[24,4,8,384]{3,2,1,0:T(8,128)} %pack.1), calls=%async_computation | async-start | bytes 2359296 | tf_op jit(solution)/shard_map/all_to_all | solution.py:262
  32.7 207.6 %all-gather.7.cloned.1.call-start = ((), (), s32[]{:S(2)}) async-start(), calls=%async_computation.5 | async-start | bytes 5308416 | tf_op jit(solution)/shard_map/all_gather | solution.py:289
  110.6 31.4 %collective-permute-start.1 = (f32[12,2,8,384]{3,2,1,0:T(8,128)S(1)}, f32[12,2,8,384]{3,2,1,0:T(8,128)S(1)}, u32[]{:S(2)}, u32[]{:S(2)}) collective-permute-start(f32[12,2,8,384]{3,2,1,0:T(8,128)S(1)} %get-tuple-element.23.refs_1_), channel_id=1, source_target_pairs={{0,16},{8,24},{16,0},{24,8},{1,17},{9,25},{17,1},{25,9},{2,18},{10... | collective-permute-start | bytes 884744 | tf_op jit(solution)/shard_map/ppermute | solution.py:228
  122.6 29.0 %collective-permute-start = (f32[12,2,8,384]{3,2,1,0:T(8,128)S(1)}, f32[12,2,8,384]{3,2,1,0:T(8,128)S(1)}, u32[]{:S(2)}, u32[]{:S(2)}) collective-permute-start(f32[12,2,8,384]{3,2,1,0:T(8,128)S(1)} %get-tuple-element.24.refs_1_), channel_id=1, source_target_pairs={{0,16},{8,24},{16,0},{24,8},{1,17},{9,25},{17,1},{25,9},{2,18},{10... | collective-permute-start | bytes 884744 | tf_op jit(solution)/shard_map/ppermute | solution.py:228
  142.0 6.3 %copy-start = (f32[2,1,192,384]{3,2,1,0:T(8,128)S(1)}, f32[2,1,192,384]{3,2,1,0:T(8,128)}, u32[]{:S(2)}) copy-start(f32[2,1,192,384]{3,2,1,0:T(8,128)} %param.4) | copy-start | bytes 1769476
  145.2 15.1 %collective-permute-start.3 = (f32[2,96,384]{2,1,0:T(8,128)S(1)}, f32[2,96,384]{2,1,0:T(8,128)S(1)}, u32[]{:S(2)}, u32[]{:S(2)}) collective-permute-start(f32[2,96,384]{2,1,0:T(8,128)S(1)} %product_other.4), channel_id=1, source_target_pairs={{0,8},{8,0},{16,24},{24,16},{1,9},{9,1},{17,25},{25,17},{2,10},{10... | collective-permute-start | bytes 884744 | tf_op jit(solution)/shard_map/ppermute | solution.py:235
  154.9 9.6 %collective-permute-start.4 = (f32[2,96,384]{2,1,0:T(8,128)S(1)}, f32[2,96,384]{2,1,0:T(8,128)S(1)}, u32[]{:S(2)}, u32[]{:S(2)}) collective-permute-start(f32[2,96,384]{2,1,0:T(8,128)S(1)} %product_other.5), channel_id=1, source_target_pairs={{0,8},{8,0},{16,24},{24,16},{1,9},{9,1},{17,25},{25,17},{2,10},{10... | collective-permute-start | bytes 884744 | tf_op jit(solution)/shard_map/ppermute | solution.py:235
  164.5 0.7 collective-permute-start.7
  216.6 23.7 %collective-permute-start.6 = (f32[12,2,8,384]{3,2,1,0:T(8,128)S(1)}, f32[12,2,8,384]{3,2,1,0:T(8,128)S(1)}, u32[]{:S(2)}, u32[]{:S(2)}) collective-permute-start(f32[12,2,8,384]{3,2,1,0:T(8,128)S(1)} %get-tuple-element.21.refs_1_), channel_id=1, source_target_pairs={{0,16},{8,24},{16,0},{24,8},{1,17},{9,25},{17,1},{25,9},{2,18},{10... | collective-permute-start | bytes 884744 | tf_op jit(solution)/shard_map/ppermute | solution.py:228
  227.7 19.2 %collective-permute-start.5 = (f32[12,2,8,384]{3,2,1,0:T(8,128)S(1)}, f32[12,2,8,384]{3,2,1,0:T(8,128)S(1)}, u32[]{:S(2)}, u32[]{:S(2)}) collective-permute-start(f32[12,2,8,384]{3,2,1,0:T(8,128)S(1)} %get-tuple-element.22.refs_1_), channel_id=1, source_target_pairs={{0,16},{8,24},{16,0},{24,8},{1,17},{9,25},{17,1},{25,9},{2,18},{10... | collective-permute-start | bytes 884744 | tf_op jit(solution)/shard_map/ppermute | solution.py:228
  250.1 27.8 %collective-permute-start.9 = (f32[2,96,384]{2,1,0:T(8,128)S(1)}, f32[2,96,384]{2,1,0:T(8,128)S(1)}, u32[]{:S(2)}, u32[]{:S(2)}) collective-permute-start(f32[2,96,384]{2,1,0:T(8,128)S(1)} %product_other.7), channel_id=1, source_target_pairs={{0,8},{8,0},{16,24},{24,16},{1,9},{9,1},{17,25},{25,17},{2,10},{10... | collective-permute-start | bytes 884744 | tf_op jit(solution)/shard_map/ppermute | solution.py:235
  272.8 9.1 %collective-permute-start.8 = (f32[2,96,384]{2,1,0:T(8,128)S(1)}, f32[2,96,384]{2,1,0:T(8,128)S(1)}, u32[]{:S(2)}, u32[]{:S(2)}) collective-permute-start(f32[2,96,384]{2,1,0:T(8,128)S(1)} %product_other.6), channel_id=1, source_target_pairs={{0,8},{8,0},{16,24},{24,16},{1,9},{9,1},{17,25},{25,17},{2,10},{10... | collective-permute-start | bytes 884744 | tf_op jit(solution)/shard_map/ppermute | solution.py:235
Sparse Core Ops, SparseCore 0:
  9.7 77.8 all-gather.4
  166.2 64.6 all-gather.6
where the time goes:
time: 294 us; the launch traced here: 290 us
  blocking collectives  95.3 us (32%)
  starting transfers between devices  79.3 us (27%)
  waiting for transfers between devices  66.7 us (23%)
  Pallas kernels  34.2 us (12%)
  between operations  13.6 us (5%)
    all_to_all x3, blocking collectives, exchange(): return lax.all_to_all(x, ('zh', 'y'), 0, 0, tiled=True)  95.3 us
    all_to_all x1, waiting for transfers between devices, exchange(): return lax.all_to_all(x, ('zh', 'y'), 0, 0, tiled=True)  30.7 us
    ppermute x4, starting transfers between devices, time_product(): other.append(lax.ppermute(part, 'zl', [(0, 1), (1, 0), (2, 3), (3, 2)]))  29.8 us
    ppermute x4, waiting for transfers between devices, time_product(): lax.ppermute(x, 'zl', [(0, 2), (1, 3), (2, 0), (3, 1)])  28 us
    ppermute x4, starting transfers between devices, time_product(): lax.ppermute(x, 'zl', [(0, 2), (1, 3), (2, 0), (3, 1)])  27 us
    pallas_call x8, Pallas kernels, product(): pl.pallas_call(lambda *refs: product_kernel(len(lefts), *refs), out_shape...  26 us
    all_to_all x1, starting transfers between devices, exchange(): return lax.all_to_all(x, ('zh', 'y'), 0, 0, tiled=True)  20 us
    ppermute x4, waiting for transfers between devices, time_product(): other.append(lax.ppermute(part, 'zl', [(0, 1), (1, 0), (2, 3), (3, 2)]))  7.95 us
  transfers between devices with their start and end apart: 13, of which 5 were waited for; matrix products, arithmetic and copies ran while one was open for 0% of the time, Pallas kernels for 10%

commit v1 on v0

--- a/solution.py
+++ b/solution.py
@@ -12,6 +12,7 @@
 
 
 CHUNKS = 2
+ZL = ("h", "l")
 VMEM = 24 * 1024 * 1024
 
 LANES = 128
@@ -73,7 +74,7 @@
     for k in range(momenta):
         where_ref[map_ref[k]] = k
     spot = [where_ref[q] for q in range(momenta)]
-    zl = lax.axis_index("zl")
+    zl = lax.axis_index(ZL)
     for lane in range(0, field_ref.shape[3], LANES):
         cut = pl.ds(lane, LANES)
         if first:
@@ -219,58 +220,32 @@
 
 
 def time_product(sigma, panel, free, tiled):
-    zl = lax.axis_index("zl")
-    turn = lambda by: lax.bitwise_xor(zl, by)
-    own_blocks = jnp.stack([zl, turn(2)])
-    other_blocks = jnp.stack([turn(1), turn(3)])
+    zl = lax.axis_index(ZL)
+    column = lax.axis_index("l")
+    per = lax.axis_size("x")
+    rows = jnp.stack([zl, lax.bitwise_xor(zl, 2)])
+    own_blocks = column * per + rows
+    other_blocks = (1 - column) * per + rows
     slabs = sigma.shape[0] // CHUNKS
     mine = [sigma[i * slabs : (i + 1) * slabs] for i in range(CHUNKS)]
-    swapped = [lax.ppermute(x, "zl", [(0, 2), (1, 3), (2, 0), (3, 1)]) for x in mine]
+    swapped = [lax.ppermute(x, ZL, [(0, 2), (1, 3), (2, 0), (3, 1)]) for x in mine]
     own, other = [], []
     for i, (left, right) in enumerate(zip(mine, swapped)):
         if own:
             right, own[-1], _ = lax.optimization_barrier((right, own[-1], part))
         pair = (left, right)
         part = product(pair, panel, other_blocks)
-        other.append(lax.ppermute(part, "zl", [(0, 1), (1, 0), (2, 3), (3, 2)]))
+        other.append(lax.ppermute(part, ZL, [(0, 1), (1, 0), (2, 3), (3, 2)]))
         own.append(product(pair, panel, own_blocks, free, i))
     return finish(own, other, sigma.shape if tiled else None)
 
 
-def pack_kernel(free_ref, greater_ref, out_ref):
-    for j in range(2):
-        out_ref[:, j] = free_ref[j]
-        out_ref[:, 2 + j] = greater_ref[j]
-
-
 def pack(free, greater):
-    _, slabs, high, cols = free.shape
-    step = slabs // 4
-    block = pl.BlockSpec((2, step, high, cols), lambda i: (0, i, 0, 0))
-    return pl.pallas_call(
-        pack_kernel,
-        out_shape=jax.ShapeDtypeStruct((slabs, 4, high, cols), jnp.float32),
-        grid=(4,),
-        in_specs=[block, block],
-        out_specs=pl.BlockSpec((step, 4, high, cols), lambda i: (i, 0, 0, 0)),
-        compiler_params=pltpu.CompilerParams(vmem_limit_bytes=VMEM),
-        name="pack",
-    )(*(pltpu.with_memory_space_constraint(x, pltpu.HBM) for x in (free, greater)))
+    return jnp.concatenate([free, greater], axis=0).swapaxes(0, 1)
 
 
 def exchange(x):
     return lax.all_to_all(x, ("zh", "y"), 0, 0, tiled=True)
-
-
-def spread(tile):
-    nx = lax.axis_size("x")
-    moves = []
-    for zl in range(lax.axis_size("zl")):
-        for x in range(nx):
-            stays = x % 2 == zl % 2
-            to = (zl, x) if stays else (zl ^ 1, x ^ 1)
-            moves.append((zl * nx + x, to[0] * nx + to[1]))
-    return lax.ppermute(tile, ("zl", "x"), moves)
 
 
 def body(g_free, g_greater_t, momentum_map, weights):
@@ -280,13 +255,11 @@
     slabs = (2, momenta, tile_rows // momenta, tile_cols)
     weights = weights.reshape(-1, 1, tile_cols)
 
-    moved = spread(free)
-    both = pack(free.reshape(slabs), greater.reshape(slabs))
-    field = exchange(both)
+    green = free
+    field = exchange(pack(free.reshape(slabs), greater.reshape(slabs)))
     mirror = None
     for sweep in range(ITERS):
-        moved = settle(moved)
-        panel = lax.all_gather(moved, ("x", "core"))
+        panel = lax.all_gather(green, ("l", "x", "core"))
         panel = pltpu.with_memory_space_constraint(panel, pltpu.HBM)
         if mirror is None:
             sigma, mirror = self_energy(momentum_map, weights, field)
@@ -296,25 +269,12 @@
         if sweep == ITERS - 1:
             return time_product(sigma, panel, free, False)[0][:, None]
         green, tiles = time_product(sigma, panel, free, True)
-        moved = spread(green)
         field = exchange(tiles)
 
 
-def settle(tile):
-    def kernel(tile_ref, out_ref):
-        out_ref[...] = tile_ref[...]
-
-    return pl.pallas_call(
-        kernel,
-        out_shape=jax.ShapeDtypeStruct(tile.shape, tile.dtype),
-        compiler_params=pltpu.CompilerParams(vmem_limit_bytes=VMEM),
-        name="settle",
-    )(tile)
-
-
 def solution(mesh):
-    fine = Mesh(mesh.devices.reshape(3, 8, 4, 4, 2), ("zh", "y", "zl", "x", "core"))
-    spec = P(None, ("zh", "y"), ("x", "core"), "zl")
+    fine = Mesh(mesh.devices.reshape(3, 8, 2, 2, 4, 2), ("zh", "y", "h", "l", "x", "core"))
+    spec = P(None, ("zh", "y"), ("x", "core"), ZL)
     return jax.shard_map(
         body, mesh=fine, in_specs=(spec, spec, P(), P()), out_specs=spec, check_vma=False
     )

time: 294 us -> 302 us (1.027); the launches traced: 290 us -> 301 us
  waiting for transfers between devices: 66.7 us -> 83.2 us
  starting transfers between devices: 79.3 us -> 63.8 us
  blocking collectives: 95.3 us -> 108 us
  Pallas kernels: 34.2 us -> 29.8 us
    all_gather x2, waiting for transfers between devices: 0.01 us -> 24.2 us  [body(): panel = lax.all_gather(green, ('l', 'x', 'core'))]
    ppermute x10 -> x8, starting transfers between devices: 59.3 us -> 43.7 us  [the longest x4 33.1 us: time_product(): lax.ppermute(x, ZL, [(0, 2), (1, 3), (2, 0), (3, 1)])]
    all_to_all x3, blocking collectives: 95.3 us -> 108 us  [exchange(): return lax.all_to_all(x, ('zh', 'y'), 0, 0, tiled=True)]
    ppermute x10 -> x8, waiting for transfers between devices: 36 us -> 29.8 us  [the longest x4 21.8 us: time_product(): lax.ppermute(x, ZL, [(0, 2), (1, 3), (2, 0), (3, 1)])]
    pallas_call x3 -> x0, Pallas kernels: 5.21 us -> none  [the longest x1 3.5 us: pack(): pl.pallas_call(pack_kernel, out_shape=jax.ShapeDtypeStruct((slabs, 4, hig...]
  transfers between devices with their start and end apart: 13 -> 11, of which waited for: 5 -> 7; matrix products, arithmetic and copies ran while one was open for 0% -> 1% of each run, Pallas kernels for 10% -> 9%
where the time goes in v1:
time: 302 us; the launch traced here: 301 us
  blocking collectives  108 us (36%)
  waiting for transfers between devices  83.2 us (28%)
  starting transfers between devices  63.8 us (21%)
  Pallas kernels  29.8 us (10%)
  between operations  13.6 us (5%)
    all_to_all x3, blocking collectives, exchange(): return lax.all_to_all(x, ('zh', 'y'), 0, 0, tiled=True)  108 us
    ppermute x4, starting transfers between devices, time_product(): lax.ppermute(x, ZL, [(0, 2), (1, 3), (2, 0), (3, 1)])  33.1 us
    all_to_all x1, waiting for transfers between devices, exchange(): return lax.all_to_all(x, ('zh', 'y'), 0, 0, tiled=True)  28.5 us
    pallas_call x8, Pallas kernels, product(): pl.pallas_call(lambda *refs: product_kernel(len(lefts), *refs), out_shape...  26 us
    all_gather x2, waiting for transfers between devices, body(): panel = lax.all_gather(green, ('l', 'x', 'core'))  24.2 us
    ppermute x4, waiting for transfers between devices, time_product(): lax.ppermute(x, ZL, [(0, 2), (1, 3), (2, 0), (3, 1)])  21.8 us
    all_to_all x1, starting transfers between devices, exchange(): return lax.all_to_all(x, ('zh', 'y'), 0, 0, tiled=True)  20.1 us
    ppermute x4, starting transfers between devices, time_product(): other.append(lax.ppermute(part, ZL, [(0, 1), (1, 0), (2, 3), (3, 2)]))  10.6 us
  transfers between devices with their start and end apart: 11, of which 7 were waited for; matrix products, arithmetic and copies ran while one was open for 1% of the time, Pallas kernels for 9%

profile of v1, /device:TPU:1, one launch (start us, length us, event | category | flops | bytes accessed | tf_op | source)
XLA Modules:
  0.0 301.3 jit_solution(14619036955546523929)
XLA Ops:
  7.3 2.4 copy_bitcast_fusion
  9.7 20.1 %all-to-all-start = ((f32[24,4,8,384]{3,2,1,0:T(8,128)}), f32[24,4,8,384]{3,2,1,0:T(8,128)S(1)}, u32[]{:S(2)}, u32[]{:S(2)}) async-start(f32[24,4,8,384]{3,2,1,0:T(8,128)} %copy_bitcast_fusion), calls=%async_computation | async-start | bytes 2359296 | tf_op jit(solution)/shard_map/all_to_all | solution.py:248
  29.9 28.5 %all-to-all-done.refs_2_ = f32[24,4,8,384]{3,2,1,0:T(8,128)S(1)} async-done(((f32[24,4,8,384]{3,2,1,0:T(8,128)}), f32[24,4,8,384]{3,2,1,0:T(8,128)S(1)}, u32[]{:S(2)}, u32[]{:S(2)}) %all-to-all-start) | async-done | bytes 1179680 | tf_op jit(solution)/shard_map/all_to_all | solution.py:248
  58.4 1.1 self_energy_first.1
  59.5 33.5 %all_to_all.20 = f32[24,2,8,384]{3,2,1,0:T(8,128)S(1)} all-to-all(f32[24,2,8,384]{3,2,1,0:T(8,128)S(1)} %get-tuple-element.13), channel_id=1, replica_groups=mesh['zh'=3,'y'=8,'h'=2,'l'=2,'x'=4,'core'=2] {'zh','y'}, dimensions={0} | all-to-all | bytes 1179648 | tf_op jit(solution)/shard_map/all_to_all | solution.py:248
  93.0 24.0 %collective-permute-start.1 = (f32[12,2,8,384]{3,2,1,0:T(8,128)S(1)}, f32[12,2,8,384]{3,2,1,0:T(8,128)S(1)}, u32[]{:S(2)}, u32[]{:S(2)}) collective-permute-start(f32[12,2,8,384]{3,2,1,0:T(8,128)S(1)} %get-tuple-element.23.refs_1_), channel_id=1, source_target_pairs={{0,16},{8,24},{16,0},{24,8},{1,17},{9,25},{17,1},{25,9},{2,18},{10... | collective-permute-start | bytes 884744 | tf_op jit(solution)/shard_map/ppermute | solution.py:231
  117.0 1.9 collective-permute-start
  119.1 10.7 %collective-permute-done.1.refs_2_ = f32[12,2,8,384]{3,2,1,0:T(8,128)S(1)} collective-permute-done((f32[12,2,8,384]{3,2,1,0:T(8,128)S(1)}, f32[12,2,8,384]{3,2,1,0:T(8,128)S(1)}, u32[]{:S(2)}, u32[]{:S(2)}) %collective-permute-start.1) | collective-permute-done | bytes 294944 | tf_op jit(solution)/shard_map/ppermute | solution.py:231
  129.9 8.5 %all-gather.5.cloned.1.call-done = f32[32,1,192,384]{3,2,1,0:T(8,128)} async-done(((f32[2,1,192,384]{3,2,1,0:T(8,128)}), f32[32,1,192,384]{3,2,1,0:T(8,128)}) %all-gather.5.cloned.1.call-update) | async-done | bytes 9437200 | tf_op jit(solution)/shard_map/all_gather | solution.py:262
  138.4 3.2 %product_other.4 = f32[2,96,384]{2,1,0:T(8,128)S(1)} custom-call(s32[2]{0:T(128)S(1)} %broadcast_add_fusion.refs_0_, f32[12,2,8,384]{3,2,1,0:T(8,128)S(1)} %get-tuple-element.23.refs_1_, f32[12,2,8,384]{3,2,1,0:T(8,128)S(1)} %collective-permute-done.1.refs_2_, f32[16,2,192,384]{3,2,1,0:T(8,128)} %bitcast.17, f32[16,2,192,384]{3,2,1,0:T(8,128)} %bitcast.18), custom_call_target="tpu_custom_call" | custom-call | tf_op jit(solution)/shard_map/product_other/pallas_call | solution.py:177
  141.6 1.9 collective-permute-start.2
  143.6 3.2 %product_own.4.refs_0_ = f32[2,96,384]{2,1,0:T(8,128)S(1)} custom-call(s32[2]{0:T(128)S(1)} %broadcast_add_fusion.1.refs_0_, f32[12,2,8,384]{3,2,1,0:T(8,128)S(1)} %get-tuple-element.23.refs_1_, f32[12,2,8,384]{3,2,1,0:T(8,128)S(1)} %collective-permute-done.1.refs_2_, f32[16,2,192,384]{3,2,1,0:T(8,128)} %bitcast.19, f32[16,2,192,384]{3,2,1,0:T(8,128)} %bitcast.20, ...), custom_call_target="tpu_custom_call" | custom-call | tf_op jit(solution)/shard_map/product_own/pallas_call | solution.py:177
  146.8 3.3 %product_other.5 = f32[2,96,384]{2,1,0:T(8,128)S(1)} custom-call(s32[2]{0:T(128)S(1)} %broadcast_add_fusion.refs_0_, f32[12,2,8,384]{3,2,1,0:T(8,128)S(1)} %get-tuple-element.24.refs_1_, f32[12,2,8,384]{3,2,1,0:T(8,128)S(1)} %collective-permute-done.refs_2_, f32[16,2,192,384]{3,2,1,0:T(8,128)} %bitcast.21, f32[16,2,192,384]{3,2,1,0:T(8,128)} %bitcast.22), custom_call_target="tpu_custom_call" | custom-call | tf_op jit(solution)/shard_map/product_other/pallas_call | solution.py:177
  150.1 3.4 %collective-permute-start.3 = (f32[2,96,384]{2,1,0:T(8,128)S(1)}, f32[2,96,384]{2,1,0:T(8,128)S(1)}, u32[]{:S(2)}, u32[]{:S(2)}) collective-permute-start(f32[2,96,384]{2,1,0:T(8,128)S(1)} %product_other.5), channel_id=1, source_target_pairs={{0,8},{8,0},{16,24},{24,16},{1,9},{9,1},{17,25},{25,17},{2,10},{10... | collective-permute-start | bytes 884744 | tf_op jit(solution)/shard_map/ppermute | solution.py:238
  153.5 3.2 %product_own.5.refs_1_ = f32[2,96,384]{2,1,0:T(8,128)S(1)} custom-call(s32[2]{0:T(128)S(1)} %broadcast_add_fusion.1.refs_0_, f32[12,2,8,384]{3,2,1,0:T(8,128)S(1)} %get-tuple-element.24.refs_1_, f32[12,2,8,384]{3,2,1,0:T(8,128)S(1)} %collective-permute-done.refs_2_, f32[16,2,192,384]{3,2,1,0:T(8,128)} %bitcast.23, f32[16,2,192,384]{3,2,1,0:T(8,128)} %bitcast.24, ...), custom_call_target="tpu_custom_call" | custom-call | tf_op jit(solution)/shard_map/product_own/pallas_call | solution.py:177
  156.7 3.6 %collective-permute-done.3.refs_3_ = f32[2,96,384]{2,1,0:T(8,128)S(1)} collective-permute-done((f32[2,96,384]{2,1,0:T(8,128)S(1)}, f32[2,96,384]{2,1,0:T(8,128)S(1)}, u32[]{:S(2)}, u32[]{:S(2)}) %collective-permute-start.3) | collective-permute-done | bytes 294944 | tf_op jit(solution)/shard_map/ppermute | solution.py:238
  160.3 0.9 finish_tiled.1
  161.2 40.4 %all_to_all.21.refs_2_ = f32[24,2,8,384]{3,2,1,0:T(8,128)S(1)} all-to-all(f32[24,2,8,384]{3,2,1,0:T(8,128)S(1)} %get-tuple-element.16), channel_id=1, replica_groups=mesh['zh'=3,'y'=8,'h'=2,'l'=2,'x'=4,'core'=2] {'zh','y'}, dimensions={0} | all-to-all | bytes 1179648 | tf_op jit(solution)/shard_map/all_to_all | solution.py:248
  201.6 1.0 self_energy_next.1
  202.6 34.2 %all_to_all.22 = f32[24,2,8,384]{3,2,1,0:T(8,128)S(1)} all-to-all(f32[24,2,8,384]{3,2,1,0:T(8,128)S(1)} %self_energy_next.1), channel_id=1, replica_groups=mesh['zh'=3,'y'=8,'h'=2,'l'=2,'x'=4,'core'=2] {'zh','y'}, dimensions={0} | all-to-all | bytes 1179648 | tf_op jit(solution)/shard_map/all_to_all | solution.py:248
  236.8 5.3 %collective-permute-start.5 = (f32[12,2,8,384]{3,2,1,0:T(8,128)S(1)}, f32[12,2,8,384]{3,2,1,0:T(8,128)S(1)}, u32[]{:S(2)}, u32[]{:S(2)}) collective-permute-start(f32[12,2,8,384]{3,2,1,0:T(8,128)S(1)} %get-tuple-element.21.refs_1_), channel_id=1, source_target_pairs={{0,16},{8,24},{16,0},{24,8},{1,17},{9,25},{17,1},{25,9},{2,18},{10... | collective-permute-start | bytes 884744 | tf_op jit(solution)/shard_map/ppermute | solution.py:231
  242.1 1.9 collective-permute-start.4
  244.0 11.1 %collective-permute-done.5.refs_2_ = f32[12,2,8,384]{3,2,1,0:T(8,128)S(1)} collective-permute-done((f32[12,2,8,384]{3,2,1,0:T(8,128)S(1)}, f32[12,2,8,384]{3,2,1,0:T(8,128)S(1)}, u32[]{:S(2)}, u32[]{:S(2)}) %collective-permute-start.5) | collective-permute-done | bytes 294944 | tf_op jit(solution)/shard_map/ppermute | solution.py:231
  255.1 15.7 %all-gather.7.cloned.1.call-done = f32[32,192,384]{2,1,0:T(8,128)} async-done(((f32[2,192,384]{2,1,0:T(8,128)}), f32[32,192,384]{2,1,0:T(8,128)}) %all-gather.7.cloned.1.call-update) | async-done | bytes 9437200 | tf_op jit(solution)/shard_map/all_gather | solution.py:262
  270.8 3.2 %product_other.6 = f32[2,96,384]{2,1,0:T(8,128)S(1)} custom-call(s32[2]{0:T(128)S(1)} %broadcast_add_fusion.refs_0_, f32[12,2,8,384]{3,2,1,0:T(8,128)S(1)} %get-tuple-element.21.refs_1_, f32[12,2,8,384]{3,2,1,0:T(8,128)S(1)} %collective-permute-done.5.refs_2_, f32[16,2,192,384]{3,2,1,0:T(8,128)} %bitcast.25, f32[16,2,192,384]{3,2,1,0:T(8,128)} %bitcast.26), custom_call_target="tpu_custom_call" | custom-call | tf_op jit(solution)/shard_map/product_other/pallas_call | solution.py:177
  274.0 3.1 %collective-permute-start.6 = (f32[2,96,384]{2,1,0:T(8,128)S(1)}, f32[2,96,384]{2,1,0:T(8,128)S(1)}, u32[]{:S(2)}, u32[]{:S(2)}) collective-permute-start(f32[2,96,384]{2,1,0:T(8,128)S(1)} %product_other.6), channel_id=1, source_target_pairs={{0,8},{8,0},{16,24},{24,16},{1,9},{9,1},{17,25},{25,17},{2,10},{10... | collective-permute-start | bytes 884744 | tf_op jit(solution)/shard_map/ppermute | solution.py:238
  277.1 3.2 %product_own.6.refs_0_ = f32[2,96,384]{2,1,0:T(8,128)S(1)} custom-call(s32[2]{0:T(128)S(1)} %broadcast_add_fusion.1.refs_0_, f32[12,2,8,384]{3,2,1,0:T(8,128)S(1)} %get-tuple-element.21.refs_1_, f32[12,2,8,384]{3,2,1,0:T(8,128)S(1)} %collective-permute-done.5.refs_2_, f32[16,2,192,384]{3,2,1,0:T(8,128)} %bitcast.27, f32[16,2,192,384]{3,2,1,0:T(8,128)} %bitcast.28, ...), custom_call_target="tpu_custom_call" | custom-call | tf_op jit(solution)/shard_map/product_own/pallas_call | solution.py:177
  280.4 3.2 %product_other.7 = f32[2,96,384]{2,1,0:T(8,128)S(1)} custom-call(s32[2]{0:T(128)S(1)} %broadcast_add_fusion.refs_0_, f32[12,2,8,384]{3,2,1,0:T(8,128)S(1)} %get-tuple-element.22.refs_1_, f32[12,2,8,384]{3,2,1,0:T(8,128)S(1)} %collective-permute-done.4.refs_2_, f32[16,2,192,384]{3,2,1,0:T(8,128)} %bitcast.29, f32[16,2,192,384]{3,2,1,0:T(8,128)} %bitcast.30), custom_call_target="tpu_custom_call" | custom-call | tf_op jit(solution)/shard_map/product_other/pallas_call | solution.py:177
  283.6 2.2 collective-permute-start.7
  285.8 3.2 %product_own.7.refs_1_ = f32[2,96,384]{2,1,0:T(8,128)S(1)} custom-call(s32[2]{0:T(128)S(1)} %broadcast_add_fusion.1.refs_0_, f32[12,2,8,384]{3,2,1,0:T(8,128)S(1)} %get-tuple-element.22.refs_1_, f32[12,2,8,384]{3,2,1,0:T(8,128)S(1)} %collective-permute-done.4.refs_2_, f32[16,2,192,384]{3,2,1,0:T(8,128)} %bitcast.31, f32[16,2,192,384]{3,2,1,0:T(8,128)} %bitcast.32, ...), custom_call_target="tpu_custom_call" | custom-call | tf_op jit(solution)/shard_map/product_own/pallas_call | solution.py:177
  289.1 4.5 %collective-permute-done.7.refs_3_ = f32[2,96,384]{2,1,0:T(8,128)S(1)} collective-permute-done((f32[2,96,384]{2,1,0:T(8,128)S(1)}, f32[2,96,384]{2,1,0:T(8,128)S(1)}, u32[]{:S(2)}, u32[]{:S(2)}) %collective-permute-start.7) | collective-permute-done | bytes 294944 | tf_op jit(solution)/shard_map/ppermute | solution.py:238
  293.5 0.9 finish.1
  (19 shorter events, 1.0 us)
Async XLA Ops:
  6.5 131.8 %all-gather.5.cloned.1.call-start = ((), (), s32[]{:S(2)}) async-start(), calls=%async_computation.4 | async-start | bytes 10027008 | tf_op jit(solution)/shard_map/all_gather | solution.py:262
  9.7 20.2 %copy-start.2 = (f32[1536]{0:T(1024)S(1)}, f32[1536]{0:T(1024)}, u32[]{:S(2)}) copy-start(f32[1536]{0:T(1024)} %param.7) | copy-start | bytes 18436
  9.7 48.7 %copy-start.1 = (s32[24]{0:T(128)S(1)}, s32[24]{0:T(128)}, u32[]{:S(2)}) copy-start(s32[24]{0:T(128)} %refs_0_.3) | copy-start | bytes 292
  9.7 48.7 %all-to-all-start = ((f32[24,4,8,384]{3,2,1,0:T(8,128)}), f32[24,4,8,384]{3,2,1,0:T(8,128)S(1)}, u32[]{:S(2)}, u32[]{:S(2)}) async-start(f32[24,4,8,384]{3,2,1,0:T(8,128)} %copy_bitcast_fusion), calls=%async_computation | async-start | bytes 2359296 | tf_op jit(solution)/shard_map/all_to_all | solution.py:248
  29.8 241.0 %all-gather.7.cloned.1.call-start = ((), (), s32[]{:S(2)}) async-start(), calls=%async_computation.5 | async-start | bytes 10027008 | tf_op jit(solution)/shard_map/all_gather | solution.py:262
  93.0 36.9 %collective-permute-start.1 = (f32[12,2,8,384]{3,2,1,0:T(8,128)S(1)}, f32[12,2,8,384]{3,2,1,0:T(8,128)S(1)}, u32[]{:S(2)}, u32[]{:S(2)}) collective-permute-start(f32[12,2,8,384]{3,2,1,0:T(8,128)S(1)} %get-tuple-element.23.refs_1_), channel_id=1, source_target_pairs={{0,16},{8,24},{16,0},{24,8},{1,17},{9,25},{17,1},{25,9},{2,18},{10... | collective-permute-start | bytes 884744 | tf_op jit(solution)/shard_map/ppermute | solution.py:231
  117.0 29.8 %collective-permute-start = (f32[12,2,8,384]{3,2,1,0:T(8,128)S(1)}, f32[12,2,8,384]{3,2,1,0:T(8,128)S(1)}, u32[]{:S(2)}, u32[]{:S(2)}) collective-permute-start(f32[12,2,8,384]{3,2,1,0:T(8,128)S(1)} %get-tuple-element.24.refs_1_), channel_id=1, source_target_pairs={{0,16},{8,24},{16,0},{24,8},{1,17},{9,25},{17,1},{25,9},{2,18},{10... | collective-permute-start | bytes 884744 | tf_op jit(solution)/shard_map/ppermute | solution.py:231
  138.4 5.2 %copy-start = (f32[2,1,192,384]{3,2,1,0:T(8,128)S(1)}, f32[2,1,192,384]{3,2,1,0:T(8,128)}, u32[]{:S(2)}) copy-start(f32[2,1,192,384]{3,2,1,0:T(8,128)} %param.4) | copy-start | bytes 1769476
  141.6 15.1 %collective-permute-start.2 = (f32[2,96,384]{2,1,0:T(8,128)S(1)}, f32[2,96,384]{2,1,0:T(8,128)S(1)}, u32[]{:S(2)}, u32[]{:S(2)}) collective-permute-start(f32[2,96,384]{2,1,0:T(8,128)S(1)} %product_other.4), channel_id=1, source_target_pairs={{0,8},{8,0},{16,24},{24,16},{1,9},{9,1},{17,25},{25,17},{2,10},{10... | collective-permute-start | bytes 884744 | tf_op jit(solution)/shard_map/ppermute | solution.py:238
  150.1 10.2 %collective-permute-start.3 = (f32[2,96,384]{2,1,0:T(8,128)S(1)}, f32[2,96,384]{2,1,0:T(8,128)S(1)}, u32[]{:S(2)}, u32[]{:S(2)}) collective-permute-start(f32[2,96,384]{2,1,0:T(8,128)S(1)} %product_other.5), channel_id=1, source_target_pairs={{0,8},{8,0},{16,24},{24,16},{1,9},{9,1},{17,25},{25,17},{2,10},{10... | collective-permute-start | bytes 884744 | tf_op jit(solution)/shard_map/ppermute | solution.py:238
  236.8 18.3 %collective-permute-start.5 = (f32[12,2,8,384]{3,2,1,0:T(8,128)S(1)}, f32[12,2,8,384]{3,2,1,0:T(8,128)S(1)}, u32[]{:S(2)}, u32[]{:S(2)}) collective-permute-start(f32[12,2,8,384]{3,2,1,0:T(8,128)S(1)} %get-tuple-element.21.refs_1_), channel_id=1, source_target_pairs={{0,16},{8,24},{16,0},{24,8},{1,17},{9,25},{17,1},{25,9},{2,18},{10... | collective-permute-start | bytes 884744 | tf_op jit(solution)/shard_map/ppermute | solution.py:231
  242.1 38.3 %collective-permute-start.4 = (f32[12,2,8,384]{3,2,1,0:T(8,128)S(1)}, f32[12,2,8,384]{3,2,1,0:T(8,128)S(1)}, u32[]{:S(2)}, u32[]{:S(2)}) collective-permute-start(f32[12,2,8,384]{3,2,1,0:T(8,128)S(1)} %get-tuple-element.22.refs_1_), channel_id=1, source_target_pairs={{0,16},{8,24},{16,0},{24,8},{1,17},{9,25},{17,1},{25,9},{2,18},{10... | collective-permute-start | bytes 884744 | tf_op jit(solution)/shard_map/ppermute | solution.py:231
  274.0 15.1 %collective-permute-start.6 = (f32[2,96,384]{2,1,0:T(8,128)S(1)}, f32[2,96,384]{2,1,0:T(8,128)S(1)}, u32[]{:S(2)}, u32[]{:S(2)}) collective-permute-start(f32[2,96,384]{2,1,0:T(8,128)S(1)} %product_other.6), channel_id=1, source_target_pairs={{0,8},{8,0},{16,24},{24,16},{1,9},{9,1},{17,25},{25,17},{2,10},{10... | collective-permute-start | bytes 884744 | tf_op jit(solution)/shard_map/ppermute | solution.py:238
  283.6 9.9 %collective-permute-start.7 = (f32[2,96,384]{2,1,0:T(8,128)S(1)}, f32[2,96,384]{2,1,0:T(8,128)S(1)}, u32[]{:S(2)}, u32[]{:S(2)}) collective-permute-start(f32[2,96,384]{2,1,0:T(8,128)S(1)} %product_other.7), channel_id=1, source_target_pairs={{0,8},{8,0},{16,24},{24,16},{1,9},{9,1},{17,25},{25,17},{2,10},{10... | collective-permute-start | bytes 884744 | tf_op jit(solution)/shard_map/ppermute | solution.py:238
Sparse Core Ops, SparseCore 0:
  9.8 128.5 all-gather.4
  161.3 109.3 all-gather.6
